TPU v7x, 256 devices: a whole 4x4x8 slice. The times are simulated.
256 devices in a mesh: dp: 4 (over x), expert: 32 (over z, y), tensor: 2 (over core).
Axes of the slice: x: 4, y: 4, z: 8, core: 2. Of those that a mesh axis runs over, the one named last changes fastest.
Arguments:
- queries: bfloat16 [8192, 4096], P(('dp', 'expert'), 'tensor'), may hold values from -8 to 8
- fresh_keys: bfloat16 [8192, 512], P(('dp', 'expert'), 'tensor'), may hold values from -6 to 6
- fresh_values: bfloat16 [8192, 512], P(('dp', 'expert'), 'tensor'), may hold values from -6 to 6
- resident_keys: bfloat16 [128, 2048, 512], P(('dp', 'expert'), None, 'tensor'), may hold values from -8 to 8
- resident_values: bfloat16 [128, 2048, 512], P(('dp', 'expert'), None, 'tensor'), may hold values from -6 to 6
- out_weight: bfloat16 [4096, 2048], P('tensor', 'dp'), may hold values from -0.5 to 0.5
- residual: bfloat16 [8192, 2048], P(('dp', 'expert')), may hold values from -23 to 23
- norm_gain: float32 [2048], replicated, may hold values from 0.1 to 1.9
- expert_ids: int32 [8192, 8], P(('dp', 'expert')), may hold values from 0 to 127, all different within a row; in each aligned block of 64 rows (0 to 63, 64 to 127, ...) at most 6 rows name the same one
- gates: float32 [8192, 8], P(('dp', 'expert')), may hold values from 0.05 to 0.5
- w_gate: bfloat16 [128, 2048, 768], P(('dp', 'expert'), None, 'tensor'), may hold values from -0.125 to 0.125
- w_up: bfloat16 [128, 2048, 768], P(('dp', 'expert'), None, 'tensor'), may hold values from -0.125 to 0.125
- w_down: bfloat16 [128, 768, 2048], P(('dp', 'expert'), 'tensor'), may hold values from -0.21875 to 0.21875
Outputs:
- mixed: bfloat16 [8192, 2048], P(('dp', 'expert'), 'tensor')
Inputs may be any that keep to these rules, and one draw needn't show every extreme that they name: `expert_ids`: within the 64 tokens of one sequence no expert is named by more than 6 tokens, a bound that some block reaches; a token names 8 different experts.
All inputs are finite; a program needn't handle non-finite values.
Results may differ from a plain program's by a relative error of at most 0.0085.
Values may be sent and summed in bfloat16 or wider, within the bound.
No kernel may reach another device: no remote copies, remote signals or barrier semaphores. Data moves between devices by JAX's collectives and lax.ppermute only.
A program may use at most 64 MiB of HBM per device.

v0:
```python
import jax
import jax.numpy as jnp
from jax import lax
from jax.sharding import PartitionSpec as P

D = 2048
HEAD_WIDTH = 128


def attend_local(queries, fresh_keys, fresh_values, resident_keys, resident_values):
    tokens_here = queries.shape[0]
    kv_here = fresh_keys.shape[1] // HEAD_WIDTH
    query_group = queries.shape[1] // HEAD_WIDTH // kv_here
    context = resident_keys.shape[1]
    query_rows = queries.reshape(tokens_here, kv_here, query_group, HEAD_WIDTH)
    joined_keys = jnp.concatenate([resident_keys[0], fresh_keys], 0).reshape(
        context + tokens_here, kv_here, HEAD_WIDTH
    )
    joined_values = jnp.concatenate([resident_values[0], fresh_values], 0).reshape(
        context + tokens_here, kv_here, HEAD_WIDTH
    )
    score = jnp.einsum(
        "tjgd,sjd->jgts", query_rows, joined_keys, preferred_element_type=jnp.float32
    ) * HEAD_WIDTH ** (-0.5)
    places = jnp.arange(context + tokens_here)
    rows = jnp.arange(tokens_here)
    allowed = (places[None, :] < context) | (places[None, :] - context <= rows[:, None])
    score = jnp.where(allowed, score, jnp.float32(-1e30))
    top_score = jnp.max(score, axis=-1, keepdims=True)
    weight = jnp.exp(score - top_score)
    probs = (weight / jnp.sum(weight, axis=-1, keepdims=True)).astype(jnp.bfloat16)
    attended = jnp.einsum(
        "jgts,sjd->tjgd", probs, joined_values, preferred_element_type=jnp.float32
    )
    return attended.reshape(tokens_here, -1).astype(jnp.bfloat16)


def expert_rows(block, gate_mat, up_mat, down_mat):
    sources, items, width = block.shape
    flat = block.reshape(sources * items, width)
    gate_part = jnp.dot(flat, gate_mat, preferred_element_type=jnp.float32)
    up_part = jnp.dot(flat, up_mat, preferred_element_type=jnp.float32)
    act = (jax.nn.silu(gate_part) * up_part).astype(jnp.bfloat16)
    result = jnp.dot(act, down_mat, preferred_element_type=jnp.float32)
    return result.reshape(sources, items, -1)


def per_device(
    queries,
    fresh_keys,
    fresh_values,
    resident_keys,
    resident_values,
    out_weight,
    residual,
    norm_gain,
    expert_ids,
    gates,
    w_gate,
    w_up,
    w_down,
):
    attended = attend_local(queries, fresh_keys, fresh_values, resident_keys, resident_values)
    partial_sum = jnp.dot(
        attended,
        lax.all_gather(out_weight, "dp", axis=1, tiled=True),
        preferred_element_type=jnp.float32,
    )
    tokens_here = residual.shape[0]
    pairs = lax.axis_size("tensor")
    half = D // pairs
    lane = lax.axis_index("tensor")
    summed = lax.psum(partial_sum.astype(jnp.bfloat16), "tensor").astype(jnp.float32)
    hidden = residual.astype(jnp.float32) + summed
    mean_square = jnp.mean(hidden * hidden, axis=-1, keepdims=True)
    normed = (hidden * lax.rsqrt(mean_square + 1e-06) * norm_gain).astype(jnp.bfloat16)
    hidden_half = lax.dynamic_slice_in_dim(hidden, lane * half, half, 1)
    owners = lax.axis_size("dp") * lax.axis_size("expert")
    top = expert_ids.shape[1]
    slots = max(2, tokens_here * top * 3 // (2 * owners))
    onehot = (expert_ids[:, :, None] == jnp.arange(owners)[None, None, :]).astype(jnp.int32)
    per_token = jnp.sum(onehot, axis=1)
    before = jnp.cumsum(per_token, axis=0) - per_token
    slot = jnp.sum(onehot * before[:, None, :], axis=-1)
    token_rows = jnp.broadcast_to(
        jnp.arange(tokens_here, dtype=jnp.int32)[:, None], expert_ids.shape
    )
    owner_rows = jnp.full((owners, slots), -1, jnp.int32).at[expert_ids, slot].set(token_rows)
    valid = owner_rows >= 0
    outgoing = jnp.where(
        valid[:, :, None], normed[jnp.maximum(owner_rows, 0)], jnp.zeros((), jnp.bfloat16)
    )
    expert_part = expert_rows(
        lax.all_to_all(outgoing, ("dp", "expert"), split_axis=0, concat_axis=0, tiled=True),
        w_gate[0],
        w_up[0],
        w_down[0],
    )
    owned = lax.psum_scatter(
        expert_part.astype(jnp.bfloat16), "tensor", scatter_dimension=2, tiled=True
    )
    returned = lax.all_to_all(owned, ("dp", "expert"), split_axis=0, concat_axis=0, tiled=True)
    picked = returned[expert_ids, slot]
    moe = jnp.sum(gates[:, :, None] * picked.astype(jnp.float32), axis=1)
    return (hidden_half + moe).astype(jnp.bfloat16)


def solution(mesh):
    return jax.shard_map(
        per_device,
        mesh=mesh,
        in_specs=(
            P(("dp", "expert"), "tensor"),
            P(("dp", "expert"), "tensor"),
            P(("dp", "expert"), "tensor"),
            P(("dp", "expert"), None, "tensor"),
            P(("dp", "expert"), None, "tensor"),
            P("tensor", "dp"),
            P(("dp", "expert"), None),
            P(),
            P(("dp", "expert"), None),
            P(("dp", "expert"), None),
            P(("dp", "expert"), None, "tensor"),
            P(("dp", "expert"), None, "tensor"),
            P(("dp", "expert"), "tensor", None),
        ),
        out_specs=P(("dp", "expert"), "tensor"),
        check_vma=False,
    )
```

profile of v0, /device:TPU:32, one launch (start us, length us, event | category | flops | bytes accessed | tf_op | source)
XLA Modules:
  0.0 379.2 jit_solution(17011101792321861209)
XLA Ops:
  7.3 1.5 copy.74
  13.3 4.6 %fusion.46 = f32[2,8,64]{2,1,0:T(8,128)S(1)} fusion(pred[64,2112]{1,0:T(8,128)(4,1)S(1)} %fusion.26, bf16[64,2,128]{2,0,1:T(8,128)(2,1)S(1)} %get-tuple-element.9, bf16[2048,2,128]{2,0,1:T(8,128)(2,1)} %copy.75, bf16[64,2,8,128]{3,2,1,0:T(8,128)(2,1)S(1)} %bitcast.97), kind=kOutput, calls=%fused_computation.69 | convolution fusion | flops 564463680 | bytes 1482752 | tf_op jit(solution)/shard_map/sub | solution.py:30
  17.9 4.9 %fusion.19 = bf16[64,2,8,128]{3,0,2,1:T(8,128)(2,1)S(1)} fusion(f32[2,8,64]{2,1,0:T(8,128)S(1)} %fusion.46, bf16[64,2,128]{2,0,1:T(8,128)(2,1)S(1)} %get-tuple-element.10, bf16[2048,2,128]{2,0,1:T(8,128)(2,1)} %copy.72, pred[64,2112]{1,0:T(8,128)(4,1)S(1)} %fusion.26, bf16[64,2,128]{2,0,1:T(8,128)(2,1)S(1)} %get-tuple-element.9, ...), kind=kOutput, calls=%fused_computation.25 | convolution fusion | flops 1122569216 | bytes 2826240 | tf_op jit(solution)/shard_map/jgts,sjd->tjgd/dot_general | solution.py:32
  25.0 22.0 %scatter_fusion = s32[128,6]{0,1:T(8,128)S(1)} fusion(s32[128,6]{0,1:T(8,128)S(1)} %broadcast_in_dim.26, s32[512]{0:T(512)S(1)} %reshape.80, s32[512]{0:T(512)S(1)} %reshape.82), kind=kCustom, calls=%fused_computation.2 | custom fusion | bytes 10240 | tf_op jit(solution)/shard_map/scatter | solution.py:88
  47.3 50.1 %all-gather.2.cloned.1.call-done = bf16[2048,2048]{1,0:T(8,128)(2,1)} async-done(((bf16[2048,512]{1,0:T(8,128)(2,1)}), bf16[2048,2048]{1,0:T(8,128)(2,1)}) %all-gather.2.cloned.1.call-update) | async-done | bytes 8388624 | tf_op jit(solution)/shard_map/all_gather | solution.py:66
  97.4 5.7 %convolution_convert_fusion.1 = bf16[64,2048]{1,0:T(8,128)(2,1)} fusion(bf16[2048,2048]{1,0:T(8,128)(2,1)} %all-gather.2.cloned.1.call-done, bf16[8,8,16,128]{3,2,1,0:T(8,128)(2,1)S(1)} %bitcast.95), kind=kOutput, calls=%fused_computation.14 | convolution fusion | flops 537001984 | bytes 8912896 | tf_op jit(solution)/shard_map/dot_general | solution.py:64
  103.5 29.8 %all-reduce.2.cloned.1.call-done = bf16[64,2048]{1,0:T(8,128)(2,1)} async-done(((bf16[64,2048]{1,0:T(8,128)(2,1)}), bf16[64,2048]{1,0:T(8,128)(2,1)}) %all-reduce.2.cloned.1.call-update) | async-done | bytes 262160 | tf_op jit(solution)/shard_map/psum | solution.py:73
  133.3 1.9 convert_add_fusion
  136.3 4.3 %gather_fusion = bf16[768,2048]{1,0:T(8,128)(2,1)} fusion(bf16[64,2048]{1,0:T(8,128)(2,1)S(1)} %multiply_convert_fusion, s32[1024]{0:T(1024)S(1)} %pad_clamp_fusion), kind=kCustom, calls=%fused_computation | custom fusion | bytes 6294528 | tf_op jit(solution)/shard_map/gather | solution.py:91
  140.6 6.3 %reshape.67 = bf16[128,6,2048]{2,1,0:T(8,128)(2,1)} reshape(bf16[768,2048]{1,0:T(8,128)(2,1)} %gather_fusion) | data formatting | bytes 6291456 | tf_op jit(solution)/shard_map/gather | solution.py:91
  146.9 2.6 broadcast_select_fusion
  149.5 111.2 %all_to_all.10 = bf16[128,6,2048]{2,1,0:T(8,128)(2,1)} all-to-all(bf16[128,6,2048]{2,1,0:T(8,128)(2,1)S(1)} %broadcast_select_fusion), channel_id=1, replica_groups=mesh['dp'=4,'expert'=32,'tensor'=2] {'dp','expert'}, dimensions={0} | all-to-all | bytes 6291456 | tf_op jit(solution)/shard_map/all_to_all | solution.py:94
  260.8 6.3 %reshape.65 = bf16[768,2048]{1,0:T(8,128)(2,1)} reshape(bf16[128,6,2048]{2,1,0:T(8,128)(2,1)} %all_to_all.10) | data formatting | bytes 6291456 | tf_op jit(solution)/shard_map/reshape | solution.py:40
  267.1 4.3 %fusion.10 = f32[768,384]{1,0:T(8,128)S(1)} fusion(bf16[768,2048]{1,0:T(8,128)(2,1)} %reshape.65, bf16[1,2048,384]{2,1,0:T(8,128)(2,1)} %param.23), kind=kOutput, calls=%fused_computation.20 | convolution fusion | flops 1207959552 | bytes 5898240 | tf_op jit(solution)/shard_map/dot_general | solution.py:41
  271.4 1.8 fusion.15
  273.5 3.5 convolution_convert_fusion
  277.0 11.5 %reduce-scatter.2.cloned.1.call-done = bf16[128,6,1024]{2,0,1:T(8,128)(2,1)} async-done(((bf16[128,6,2048]{2,0,1:T(8,128)(2,1)}), bf16[128,6,1024]{2,0,1:T(8,128)(2,1)}) %reduce-scatter.2.cloned.1.call-update) | async-done | bytes 1572880 | tf_op jit(solution)/shard_map/reduce_scatter | solution.py:99
  288.4 3.6 copy.86
  292.1 14.3 %all-to-all-start.1 = ((bf16[128,6,1024]{2,1,0:T(8,128)(2,1)}), bf16[128,6,1024]{2,1,0:T(8,128)(2,1)}, u32[]{:S(2)}, u32[]{:S(2)}) async-start(bf16[128,6,1024]{2,1,0:T(8,128)(2,1)} %copy.86), calls=%async_computation.2 | async-start | bytes 4194304 | tf_op jit(solution)/shard_map/all_to_all | solution.py:102
  306.7 52.1 %all-to-all-done.1 = bf16[128,6,1024]{2,1,0:T(8,128)(2,1)} async-done(((bf16[128,6,1024]{2,1,0:T(8,128)(2,1)}), bf16[128,6,1024]{2,1,0:T(8,128)(2,1)}, u32[]{:S(2)}, u32[]{:S(2)}) %all-to-all-start.1) | async-done | bytes 1572896 | tf_op jit(solution)/shard_map/all_to_all | solution.py:102
  358.8 2.5 copy.88
  361.2 7.9 %gather_fusion.1 = bf16[512,1024]{1,0:T(8,128)(2,1)} fusion(bf16[128,6,1024]{2,0,1:T(8,128)(2,1)S(1)} %copy.88, s32[512]{0:T(512)S(1)} %reshape.74), kind=kCustom, calls=%fused_computation.1 | custom fusion | bytes 2101248 | tf_op jit(solution)/shard_map/gather | solution.py:103
  369.1 1.9 fusion.6
  371.0 1.6 add_convert_fusion
  (61 shorter events, 9.4 us)
Async XLA Ops:
  6.5 266.9 %copy-start = (bf16[1,384,2048]{2,1,0:T(8,128)(2,1)S(1)}, bf16[1,384,2048]{2,1,0:T(8,128)(2,1)}, u32[]{:S(2)}) copy-start(bf16[1,384,2048]{2,1,0:T(8,128)(2,1)} %param.25) | copy-start | bytes 4718596
  6.5 90.8 %all-gather.2.cloned.1.call-start = ((), (), s32[]{:S(2)}) async-start(), calls=%async_computation.3 | async-start | bytes 10485760 | tf_op jit(solution)/shard_map/all_gather | solution.py:66
  7.3 3.0 copy-start.4
  7.3 126.1 %all-reduce.2.cloned.1.call-start = ((), (), s32[]{:S(2)}) async-start(), calls=%async_computation.4 | async-start | bytes 524288 | tf_op jit(solution)/shard_map/psum | solution.py:73
  10.3 2.8 copy-start.5
  10.3 2.8 copy-start.6
  13.3 4.7 %copy-start.2 = (bf16[2048,2,128]{2,0,1:T(8,128)(2,1)S(1)}, bf16[2048,2,128]{2,0,1:T(8,128)(2,1)}, u32[]{:S(2)}) copy-start(bf16[2048,2,128]{2,0,1:T(8,128)(2,1)} %copy.75) | copy-start | bytes 3145732
  17.9 5.1 %copy-start.7 = (s32[64,8]{0,1:T(8,128)S(1)}, s32[64,8]{0,1:T(8,128)}, u32[]{:S(2)}) copy-start(s32[64,8]{0,1:T(8,128)} %param.21) | copy-start | bytes 6148
  97.4 35.9 %copy-start.3 = (bf16[64,2048]{1,0:T(8,128)(2,1)S(1)}, bf16[64,2048]{1,0:T(8,128)(2,1)}, u32[]{:S(2)}) copy-start(bf16[64,2048]{1,0:T(8,128)(2,1)} %param.19) | copy-start | bytes 786436
  97.4 37.9 %copy-start.8 = (f32[2048]{0:T(1024)S(1)}, f32[2048]{0:T(1024)}, u32[]{:S(2)}) copy-start(f32[2048]{0:T(1024)} %param.20) | copy-start | bytes 24580
  103.1 185.3 %reduce-scatter.2.cloned.1.call-start = ((), (), s32[]{:S(2)}) async-start(), calls=%async_computation.5 | async-start | bytes 4718592 | tf_op jit(solution)/shard_map/reduce_scatter | solution.py:99
  267.1 4.3 %copy-start.1 = (bf16[768,2048]{1,0:T(8,128)(2,1)S(1)}, bf16[768,2048]{1,0:T(8,128)(2,1)}, u32[]{:S(2)}) copy-start(bf16[768,2048]{1,0:T(8,128)(2,1)} %reshape.65) | copy-start | bytes 9437188
  267.1 4.3 %copy-start.10 = (bf16[1,2048,384]{2,1,0:T(8,128)(2,1)S(1)}, bf16[1,2048,384]{2,1,0:T(8,128)(2,1)}, u32[]{:S(2)}) copy-start(bf16[1,2048,384]{2,1,0:T(8,128)(2,1)} %param.24) | copy-start | bytes 4718596
  292.1 14.5 %copy-start.9 = (f32[64,8]{0,1:T(8,128)S(1)}, f32[64,8]{0,1:T(8,128)}, u32[]{:S(2)}) copy-start(f32[64,8]{0,1:T(8,128)} %param.22) | copy-start | bytes 6148
  292.1 66.7 %all-to-all-start.1 = ((bf16[128,6,1024]{2,1,0:T(8,128)(2,1)}), bf16[128,6,1024]{2,1,0:T(8,128)(2,1)}, u32[]{:S(2)}, u32[]{:S(2)}) async-start(bf16[128,6,1024]{2,1,0:T(8,128)(2,1)} %copy.86), calls=%async_computation.2 | async-start | bytes 4194304 | tf_op jit(solution)/shard_map/all_to_all | solution.py:102
Sparse Core Ops, SparseCore 0:
  9.1 88.1 all-gather.1
  103.2 30.0 all-reduce.1
  277.1 11.3 reduce-scatter.1
where the time goes:
time: 380 us; the launch traced here: 379 us
  waiting for transfers between devices  144 us (38%)
  blocking collectives  111 us (29%)
  local copies, waits for them, and re-layouts  60 us (16%)
  matrix products  24.9 us (7%)
  starting transfers between devices  14.6 us (4%)
  between operations  13.4 us (4%)
  other arithmetic  10.8 us (3%)
    all_to_all x1, blocking collectives, per_device(): lax.all_to_all(outgoing, ('dp', 'expert'), split_axis=0, concat_axis=0, t...  111 us
    all_to_all x1, waiting for transfers between devices, per_device(): lax.all_to_all(owned, ('dp', 'expert'), split_axis=0, concat_axis=0, tile...  52.1 us
    all_gather x1, waiting for transfers between devices, per_device(): lax.all_gather(out_weight, 'dp', axis=1, tiled=True)  50.1 us
    psum x1, waiting for transfers between devices, per_device(): lax.psum(partial_sum.astype(jnp.bfloat16), 'tensor').astype(jnp.float32)  29.8 us
    scatter x1, local copies, waits for them, and re-layouts, per_device(): jnp.full((owners, slots), -1, jnp.int32).at[expert_ids, slot]  22 us
    all_to_all x1, starting transfers between devices, per_device(): lax.all_to_all(owned, ('dp', 'expert'), split_axis=0, concat_axis=0, tile...  14.3 us
    reduce_scatter x1, waiting for transfers between devices, per_device(): lax.psum_scatter(expert_part.astype(jnp.bfloat16), 'tensor', scatter_dime...  11.5 us
    gather x2, local copies, waits for them, and re-layouts, per_device(): normed[jnp.maximum(owner_rows, 0)]  10.5 us
  transfers between devices with their start and end apart: 4, of which 4 were waited for; matrix products, arithmetic and copies ran while one was open for 11% of the time, Pallas kernels for 0%

commit v1 on v0

--- a/solution.py
+++ b/solution.py
@@ -61,10 +61,15 @@
     w_down,
 ):
     attended = attend_local(queries, fresh_keys, fresh_values, resident_keys, resident_values)
+
+    def spread_tasks_all(in_array):
+        clean = jax.lax.all_to_all(
+            jnp.stack([in_array for _ in range(jax.lax.axis_size("dp"))], 0), "dp", 0, 0
+        )
+        return jnp.concatenate(clean, 1)
+
     partial_sum = jnp.dot(
-        attended,
-        lax.all_gather(out_weight, "dp", axis=1, tiled=True),
-        preferred_element_type=jnp.float32,
+        attended, spread_tasks_all(out_weight), preferred_element_type=jnp.float32
     )
     tokens_here = residual.shape[0]
     pairs = lax.axis_size("tensor")

time: 380 us -> 400 us (1.053)
  local copies, waits for them, and re-layouts: 60 us -> 70.2 us
  starting transfers between devices: 14.6 us -> 20 us
    all_to_all x0 -> x1, waiting for transfers between devices: none -> 53.9 us  [spread_tasks_all(): jax.lax.all_to_all(jnp.stack([in_array for _ in range(jax.lax.axis_size('...]
    all_gather x1 -> x0, waiting for transfers between devices: 50.1 us -> none  [per_device(): lax.all_gather(out_weight, 'dp', axis=1, tiled=True)]
    another operation x0 -> x1, local copies, waits for them, and re-layouts: none -> 5.89 us  [spread_tasks_all(): jnp.stack([in_array for _ in range(jax.lax.axis_size('dp'))], 0)]
    all_to_all x0 -> x1, starting transfers between devices: none -> 5.65 us  [spread_tasks_all(): jax.lax.all_to_all(jnp.stack([in_array for _ in range(jax.lax.axis_size('...]
    unnamed x27 -> x28, local copies, waits for them, and re-layouts: 3.26 us -> 7.36 us
  transfers between devices with their start and end apart: 4 -> 4, of which waited for: 4 -> 4; matrix products, arithmetic and copies ran while one was open for 11% -> 10% of each run, Pallas kernels for 0% -> 0%
where the time goes in v1:
time: 400 us; the launch traced here: 399 us
  waiting for transfers between devices  147 us (37%)
  blocking collectives  111 us (28%)
  local copies, waits for them, and re-layouts  70.2 us (18%)
  matrix products  26 us (6%)
  starting transfers between devices  20 us (5%)
  between operations  13.7 us (3%)
  other arithmetic  10.8 us (3%)
    all_to_all x1, blocking collectives, per_device(): lax.all_to_all(outgoing, ('dp', 'expert'), split_axis=0, concat_axis=0, t...  111 us
    all_to_all x1, waiting for transfers between devices, spread_tasks_all(): jax.lax.all_to_all(jnp.stack([in_array for _ in range(jax.lax.axis_size('...  53.9 us
    all_to_all x1, waiting for transfers between devices, per_device(): lax.all_to_all(owned, ('dp', 'expert'), split_axis=0, concat_axis=0, tile...  52.1 us
    psum x1, waiting for transfers between devices, per_device(): lax.psum(partial_sum.astype(jnp.bfloat16), 'tensor').astype(jnp.float32)  29.7 us
    scatter x1, local copies, waits for them, and re-layouts, per_device(): jnp.full((owners, slots), -1, jnp.int32).at[expert_ids, slot]  22.2 us
    all_to_all x1, starting transfers between devices, per_device(): lax.all_to_all(owned, ('dp', 'expert'), split_axis=0, concat_axis=0, tile...  14.3 us
    reduce_scatter x1, waiting for transfers between devices, per_device(): lax.psum_scatter(expert_part.astype(jnp.bfloat16), 'tensor', scatter_dime...  11.5 us
    gather x2, local copies, waits for them, and re-layouts, per_device(): normed[jnp.maximum(owner_rows, 0)]  10.5 us
  transfers between devices with their start and end apart: 4, of which 4 were waited for; matrix products, arithmetic and copies ran while one was open for 10% of the time, Pallas kernels for 0%

profile of v1, /device:TPU:32, one launch (start us, length us, event | category | flops | bytes accessed | tf_op | source)
XLA Modules:
  0.0 399.2 jit_solution(9512298692952138060)
XLA Ops:
  6.5 4.1 %copy.82 = bf16[2048,512]{0,1:T(8,128)(2,1)} copy(bf16[2048,512]{1,0:T(8,128)(2,1)} %param.18) | data formatting | bytes 4194304 | tf_op args[5]
  10.6 5.9 %stack.2 = bf16[4,2048,512]{1,2,0:T(8,128)(2,1)} broadcast(bf16[2048,512]{0,1:T(8,128)(2,1)} %copy.82), dimensions={1,2} | broadcast | bytes 10485760 | tf_op jit(solution)/shard_map/stack | solution.py:67
  16.5 5.7 %all-to-all-start = ((bf16[4,2048,512]{1,2,0:T(8,128)(2,1)}), bf16[4,2048,512]{1,2,0:T(8,128)(2,1)}, u32[]{:S(2)}, u32[]{:S(2)}) async-start(bf16[4,2048,512]{1,2,0:T(8,128)(2,1)} %stack.2), calls=%async_computation | async-start | bytes 16777216 | tf_op jit(solution)/shard_map/all_to_all | solution.py:66
  28.2 4.6 %fusion.46 = f32[2,8,64]{2,1,0:T(8,128)S(1)} fusion(pred[64,2112]{1,0:T(8,128)(4,1)S(1)} %fusion.26, bf16[64,2,128]{2,0,1:T(8,128)(2,1)S(1)} %get-tuple-element.9, bf16[2048,2,128]{2,0,1:T(8,128)(2,1)} %copy.78, bf16[64,2,8,128]{3,2,1,0:T(8,128)(2,1)S(1)} %bitcast.100), kind=kOutput, calls=%fused_computation.69 | convolution fusion | flops 564463680 | bytes 1482752 | tf_op jit(solution)/shard_map/sub | solution.py:30
  32.8 4.9 %fusion.19 = bf16[64,2,8,128]{3,0,2,1:T(8,128)(2,1)S(1)} fusion(f32[2,8,64]{2,1,0:T(8,128)S(1)} %fusion.46, bf16[64,2,128]{2,0,1:T(8,128)(2,1)S(1)} %get-tuple-element.10, bf16[2048,2,128]{2,0,1:T(8,128)(2,1)} %copy.75, pred[64,2112]{1,0:T(8,128)(4,1)S(1)} %fusion.26, bf16[64,2,128]{2,0,1:T(8,128)(2,1)S(1)} %get-tuple-element.9, ...), kind=kOutput, calls=%fused_computation.25 | convolution fusion | flops 1122569216 | bytes 2826240 | tf_op jit(solution)/shard_map/jgts,sjd->tjgd/dot_general | solution.py:32
  39.9 22.2 %scatter_fusion = s32[128,6]{0,1:T(8,128)S(1)} fusion(s32[128,6]{0,1:T(8,128)S(1)} %broadcast_in_dim.26, s32[512]{0:T(512)S(1)} %reshape.90, s32[512]{0:T(512)S(1)} %reshape.92), kind=kCustom, calls=%fused_computation.2 | custom fusion | bytes 10240 | tf_op jit(solution)/shard_map/scatter | solution.py:93
  62.3 53.9 %all-to-all-done = bf16[4,2048,512]{1,2,0:T(8,128)(2,1)} async-done(((bf16[4,2048,512]{1,2,0:T(8,128)(2,1)}), bf16[4,2048,512]{1,2,0:T(8,128)(2,1)}, u32[]{:S(2)}, u32[]{:S(2)}) %all-to-all-start) | async-done | bytes 8388640 | tf_op jit(solution)/shard_map/all_to_all | solution.py:66
  116.3 6.8 %convolution_convert_fusion.1 = bf16[64,2048]{1,0:T(8,128)(2,1)} fusion(bf16[2048,2048]{0,1:T(8,128)(2,1)} %bitcast.9, bf16[8,8,16,128]{3,2,1,0:T(8,128)(2,1)S(1)} %bitcast.98), kind=kOutput, calls=%fused_computation.14 | convolution fusion | flops 537001984 | bytes 8912896 | tf_op jit(solution)/shard_map/dot_general | solution.py:71
  123.3 29.7 %all-reduce.2.cloned.1.call-done = bf16[64,2048]{1,0:T(8,128)(2,1)} async-done(((bf16[64,2048]{1,0:T(8,128)(2,1)}), bf16[64,2048]{1,0:T(8,128)(2,1)}) %all-reduce.2.cloned.1.call-update) | async-done | bytes 262160 | tf_op jit(solution)/shard_map/psum | solution.py:78
  153.0 1.9 convert_add_fusion
  156.1 4.3 %gather_fusion = bf16[768,2048]{1,0:T(8,128)(2,1)} fusion(bf16[64,2048]{1,0:T(8,128)(2,1)S(1)} %multiply_convert_fusion, s32[1024]{0:T(1024)S(1)} %pad_clamp_fusion), kind=kCustom, calls=%fused_computation | custom fusion | bytes 6294528 | tf_op jit(solution)/shard_map/gather | solution.py:96
  160.3 6.3 %reshape.77 = bf16[128,6,2048]{2,1,0:T(8,128)(2,1)} reshape(bf16[768,2048]{1,0:T(8,128)(2,1)} %gather_fusion) | data formatting | bytes 6291456 | tf_op jit(solution)/shard_map/gather | solution.py:96
  166.6 2.6 broadcast_select_fusion
  169.2 111.2 %all_to_all.15 = bf16[128,6,2048]{2,1,0:T(8,128)(2,1)} all-to-all(bf16[128,6,2048]{2,1,0:T(8,128)(2,1)S(1)} %broadcast_select_fusion), channel_id=1, replica_groups=mesh['dp'=4,'expert'=32,'tensor'=2] {'dp','expert'}, dimensions={0} | all-to-all | bytes 6291456 | tf_op jit(solution)/shard_map/all_to_all | solution.py:99
  280.5 6.3 %reshape.75 = bf16[768,2048]{1,0:T(8,128)(2,1)} reshape(bf16[128,6,2048]{2,1,0:T(8,128)(2,1)} %all_to_all.15) | data formatting | bytes 6291456 | tf_op jit(solution)/shard_map/reshape | solution.py:40
  286.8 4.3 %fusion.10 = f32[768,384]{1,0:T(8,128)S(1)} fusion(bf16[768,2048]{1,0:T(8,128)(2,1)} %reshape.75, bf16[1,2048,384]{2,1,0:T(8,128)(2,1)} %param.23), kind=kOutput, calls=%fused_computation.20 | convolution fusion | flops 1207959552 | bytes 5898240 | tf_op jit(solution)/shard_map/dot_general | solution.py:41
  293.2 3.5 convolution_convert_fusion
  296.7 11.5 %reduce-scatter.2.cloned.1.call-done = bf16[128,6,1024]{2,0,1:T(8,128)(2,1)} async-done(((bf16[128,6,2048]{2,0,1:T(8,128)(2,1)}), bf16[128,6,1024]{2,0,1:T(8,128)(2,1)}) %reduce-scatter.2.cloned.1.call-update) | async-done | bytes 1572880 | tf_op jit(solution)/shard_map/reduce_scatter | solution.py:104
  308.2 3.6 copy.90
  311.8 14.3 %all-to-all-start.2 = ((bf16[128,6,1024]{2,1,0:T(8,128)(2,1)}), bf16[128,6,1024]{2,1,0:T(8,128)(2,1)}, u32[]{:S(2)}, u32[]{:S(2)}) async-start(bf16[128,6,1024]{2,1,0:T(8,128)(2,1)} %copy.90), calls=%async_computation.3 | async-start | bytes 4194304 | tf_op jit(solution)/shard_map/all_to_all | solution.py:107
  326.4 52.1 %all-to-all-done.2 = bf16[128,6,1024]{2,1,0:T(8,128)(2,1)} async-done(((bf16[128,6,1024]{2,1,0:T(8,128)(2,1)}), bf16[128,6,1024]{2,1,0:T(8,128)(2,1)}, u32[]{:S(2)}, u32[]{:S(2)}) %all-to-all-start.2) | async-done | bytes 1572896 | tf_op jit(solution)/shard_map/all_to_all | solution.py:107
  378.4 2.5 copy.92
  380.9 7.9 %gather_fusion.1 = bf16[512,1024]{1,0:T(8,128)(2,1)} fusion(bf16[128,6,1024]{2,0,1:T(8,128)(2,1)S(1)} %copy.92, s32[512]{0:T(512)S(1)} %reshape.84), kind=kCustom, calls=%fused_computation.1 | custom fusion | bytes 2101248 | tf_op jit(solution)/shard_map/gather | solution.py:108
  388.8 1.9 fusion.6
  (62 shorter events, 13.5 us)
Async XLA Ops:
  6.5 286.7 %copy-start = (bf16[1,384,2048]{2,1,0:T(8,128)(2,1)S(1)}, bf16[1,384,2048]{2,1,0:T(8,128)(2,1)}, u32[]{:S(2)}) copy-start(bf16[1,384,2048]{2,1,0:T(8,128)(2,1)} %param.25) | copy-start | bytes 4718596
  16.5 99.7 %all-to-all-start = ((bf16[4,2048,512]{1,2,0:T(8,128)(2,1)}), bf16[4,2048,512]{1,2,0:T(8,128)(2,1)}, u32[]{:S(2)}, u32[]{:S(2)}) async-start(bf16[4,2048,512]{1,2,0:T(8,128)(2,1)} %stack.2), calls=%async_computation | async-start | bytes 16777216 | tf_op jit(solution)/shard_map/all_to_all | solution.py:66
  22.2 2.9 copy-start.4
  22.2 130.8 %all-reduce.2.cloned.1.call-start = ((), (), s32[]{:S(2)}) async-start(), calls=%async_computation.4 | async-start | bytes 524288 | tf_op jit(solution)/shard_map/psum | solution.py:78
  25.1 2.9 copy-start.5
  25.2 2.9 copy-start.6
  28.2 4.7 %copy-start.2 = (bf16[2048,2,128]{2,0,1:T(8,128)(2,1)S(1)}, bf16[2048,2,128]{2,0,1:T(8,128)(2,1)}, u32[]{:S(2)}) copy-start(bf16[2048,2,128]{2,0,1:T(8,128)(2,1)} %copy.78) | copy-start | bytes 3145732
  32.8 5.1 %copy-start.7 = (s32[64,8]{0,1:T(8,128)S(1)}, s32[64,8]{0,1:T(8,128)}, u32[]{:S(2)}) copy-start(s32[64,8]{0,1:T(8,128)} %param.21) | copy-start | bytes 6148
  116.3 36.8 %copy-start.3 = (bf16[64,2048]{1,0:T(8,128)(2,1)S(1)}, bf16[64,2048]{1,0:T(8,128)(2,1)}, u32[]{:S(2)}) copy-start(bf16[64,2048]{1,0:T(8,128)(2,1)} %param.19) | copy-start | bytes 786436
  116.3 38.7 %copy-start.8 = (f32[2048]{0:T(1024)S(1)}, f32[2048]{0:T(1024)}, u32[]{:S(2)}) copy-start(f32[2048]{0:T(1024)} %param.20) | copy-start | bytes 24580
  123.1 185.1 %reduce-scatter.2.cloned.1.call-start = ((), (), s32[]{:S(2)}) async-start(), calls=%async_computation.5 | async-start | bytes 4718592 | tf_op jit(solution)/shard_map/reduce_scatter | solution.py:104
  286.8 4.3 %copy-start.1 = (bf16[768,2048]{1,0:T(8,128)(2,1)S(1)}, bf16[768,2048]{1,0:T(8,128)(2,1)}, u32[]{:S(2)}) copy-start(bf16[768,2048]{1,0:T(8,128)(2,1)} %reshape.75) | copy-start | bytes 9437188
  286.8 4.3 %copy-start.10 = (bf16[1,2048,384]{2,1,0:T(8,128)(2,1)S(1)}, bf16[1,2048,384]{2,1,0:T(8,128)(2,1)}, u32[]{:S(2)}) copy-start(bf16[1,2048,384]{2,1,0:T(8,128)(2,1)} %param.24) | copy-start | bytes 4718596
  311.8 14.5 %copy-start.9 = (f32[64,8]{0,1:T(8,128)S(1)}, f32[64,8]{0,1:T(8,128)}, u32[]{:S(2)}) copy-start(f32[64,8]{0,1:T(8,128)} %param.22) | copy-start | bytes 6148
  311.8 66.6 %all-to-all-start.2 = ((bf16[128,6,1024]{2,1,0:T(8,128)(2,1)}), bf16[128,6,1024]{2,1,0:T(8,128)(2,1)}, u32[]{:S(2)}, u32[]{:S(2)}) async-start(bf16[128,6,1024]{2,1,0:T(8,128)(2,1)} %copy.90), calls=%async_computation.3 | async-start | bytes 4194304 | tf_op jit(solution)/shard_map/all_to_all | solution.py:107
Sparse Core Ops, SparseCore 0:
  123.2 29.7 all-reduce.1
  296.8 11.3 reduce-scatter.1
